TPU v7x, 32 devices: a whole 2x2x4 slice. The times are simulated.
32 devices in a mesh: band: 8 (over z, y), pair: 4 (over x, core).
Axes of the slice: x: 2, y: 2, z: 4, core: 2. Of those that a mesh axis runs over, the one named last changes fastest.
Arguments:
- orbitals: bfloat16 [32, 262144], P(('band', 'pair')), may hold values from -64 to 64
- partners: int32 [32, 3], P(('band', 'pair')), may hold values from -1 to 31, as said below
Outputs:
- gradient: float32 [32, 262144], P(None, ('band', 'pair'))
Inputs may be any that keep to these rules, and one draw needn't show every extreme that they name: `partners`: slot k of orbital i holds either -1 or i XOR (4 * 2**k); j is listed by i exactly when i is listed by j.
All inputs are finite; a program needn't handle non-finite values.
Results may differ from a plain program's by a relative error of at most 0.0008.
The roundings to bfloat16 on the way count: a program that leaves them out, or rounds other values in their place, can miss the bound.
Values may be sent and summed in bfloat16 or wider, within the bound.
A program may use at most 64 MiB of HBM per device.

v0:
```python
import math
import jax
import jax.numpy as jnp
from jax import lax
from jax.sharding import PartitionSpec as P

NG = 64
PARTNERS = 3
NG3 = 262144
screening = 0.05


def partner(value, axis, distance):
    mask = 2**distance
    pairs = [(source, source ^ mask) for source in range(lax.axis_size(axis))]
    return lax.ppermute(value, axis, pairs)


def sine_table(size):
    index = jnp.arange(size, dtype=jnp.int32) + 1
    product = index[:, None] * index[None, :] % (2 * (size + 1))
    angle = math.pi * product.astype(jnp.float32) / (size + 1)
    return jnp.sqrt(jnp.float32(2.0 / (size + 1))) * jnp.sin(angle)


def eigen_sum(size):
    steps = jnp.arange(size, dtype=jnp.float32) + 1.0
    lam = 2.0 - 2.0 * jnp.cos(math.pi * steps / (size + 1))
    total = lam[:, None, None] + lam[None, :, None] + lam[None, None, :] + screening
    return total.reshape(size, size * size)


def sine_transform(field, table, doubled):
    size = table.shape[0]
    highest = lax.Precision.HIGHEST
    field = jnp.dot(table, field, precision=highest)
    field = jnp.dot(field.reshape(-1, 2 * size), doubled, precision=highest)
    field = jnp.einsum("ky,xyz->xkz", table, field.reshape(size, size, size), precision=highest)
    return field.reshape(size, size * size)


def on_device(orbitals, partners):
    table = sine_table(NG)
    doubled = jnp.kron(jnp.eye(2, dtype=jnp.float32), table)
    denom = eigen_sum(NG)

    def solved(density):
        return sine_transform(sine_transform(density, table, doubled) / denom, table, doubled)

    def nothing(density):
        return jnp.zeros_like(density)

    own = orbitals.reshape(NG, NG * NG).astype(jnp.float32)
    live = partners[0] >= 0
    total = jnp.zeros((NG, NG * NG), jnp.float32)
    for slot in range(PARTNERS):
        arrived = partner(orbitals, "band", slot)
        other = arrived.reshape(NG, NG * NG).astype(jnp.float32)
        density = own * other
        potential = lax.cond(live[slot], solved, nothing, density)
        term = lax.optimization_barrier((potential * other).astype(jnp.bfloat16))
        total = total + jnp.where(live[slot], term.astype(jnp.float32), 0.0)
    applied = total.astype(jnp.bfloat16)
    band_count = lax.axis_size("band")
    pair_count = lax.axis_size("pair")
    cells = NG3 // (band_count * pair_count)
    layout = (1, 1, band_count, pair_count, cells)
    first = orbitals.reshape(layout)
    second = applied.reshape(layout)
    phi_slab, applied_slab = (
        lax.all_to_all(
            lax.all_to_all(first, "band", split_axis=2, concat_axis=0, tiled=True),
            "pair",
            split_axis=3,
            concat_axis=1,
            tiled=True,
        ),
        lax.all_to_all(
            lax.all_to_all(second, "band", split_axis=2, concat_axis=0, tiled=True),
            "pair",
            split_axis=3,
            concat_axis=1,
            tiled=True,
        ),
    )
    count = band_count * pair_count
    phi_slab = phi_slab.reshape(count, cells)
    applied_slab = applied_slab.reshape(count, cells)
    partial_intersection = lax.dot_general(
        phi_slab, applied_slab, (((1,), (1,)), ((), ())), preferred_element_type=jnp.float32
    )
    intersection = lax.psum(partial_intersection * (1.0 / NG3), ("band", "pair"))
    removed = lax.dot_general(
        intersection,
        phi_slab.astype(jnp.float32),
        (((0,), (0,)), ((), ())),
        precision=lax.Precision.HIGHEST,
    )
    return applied_slab.astype(jnp.float32) - removed


def solution(mesh):
    placed = (P(("band", "pair"), None), P(("band", "pair"), None))
    return jax.shard_map(
        on_device, mesh=mesh, in_specs=placed, out_specs=P(None, ("band", "pair")), check_vma=False
    )
```

profile of v0, /device:TPU:0, one launch (start us, length us, event | category | flops | bytes accessed | tf_op | source)
XLA Modules:
  0.0 283.4 jit_solution(6487296302066174337)
XLA Ops:
  0.0 3.1 %collective-permute-start.1 = (bf16[1,262144]{1,0:T(2,128)(2,1)}, bf16[1,262144]{1,0:T(2,128)(2,1)}, u32[]{:S(2)}, u32[]{:S(2)}) collective-permute-start(bf16[1,262144]{1,0:T(2,128)(2,1)} %param.8), channel_id=1, source_target_pairs={{0,8},{4,12},{8,0},{12,4},{16,24},{20,28},{24,16},{28,20},{1,9},{5... | collective-permute-start | bytes 1572872 | tf_op jit(solution)/shard_map/ppermute | solution.py:16
  3.1 1.5 collective-permute-start
  4.6 2.6 collective-permute-start.2
  7.2 11.9 %reduce.4 = bf16[262144]{0:T(1024)(128)(2,1)S(1)} reduce(bf16[1,262144]{1,0:T(2,128)(2,1)} %param.8, bf16[]{:T(256)} %constant.51), dimensions={0}, to_apply=%param.8.reduce_sub_computation | reduce | bytes 1048578 | tf_op args[0]
  20.0 4.5 %all-to-all-start.2 = ((bf16[1,1,8,4,8192]{4,3,1,0,2:T(4,128)(2,1)}), bf16[1,1,8,4,8192]{4,3,1,0,2:T(4,128)(2,1)}, u32[]{:S(2)}, u32[]{:S(2)}) async-start(bf16[1,1,8,4,8192]{4,3,1,0,2:T(4,128)(2,1)} %reshape.218), calls=%async_computation.2 | async-start | bytes 1048576 | tf_op jit(solution)/shard_map/all_to_all | solution.py:72
  24.6 9.7 %convert_reduce_fusion.3 = f32[262144]{0:T(1024)} fusion(bf16[1,262144]{1,0:T(2,128)(2,1)S(1)} %copy-done.1), kind=kLoop, calls=%fused_computation.30 | loop fusion | flops 262144 | bytes 1572864 | tf_op jit(solution)/shard_map/convert_element_type | solution.py:53
  35.4 1.7 add.210
  37.2 1.5 reshape.220
  42.3 6.1 %collective-permute-done.1 = bf16[1,262144]{1,0:T(2,128)(2,1)} collective-permute-done((bf16[1,262144]{1,0:T(2,128)(2,1)}, bf16[1,262144]{1,0:T(2,128)(2,1)}, u32[]{:S(2)}, u32[]{:S(2)}) %collective-permute-start.1) | collective-permute-done | bytes 524320 | tf_op jit(solution)/shard_map/ppermute | solution.py:16
  48.4 9.7 %convert_reduce_fusion.1 = f32[262144]{0:T(1024)S(1)} fusion(bf16[1,262144]{1,0:T(2,128)(2,1)} %collective-permute-done.1), kind=kLoop, calls=%fused_computation.28 | loop fusion | flops 262144 | bytes 1572864 | tf_op jit(solution)/shard_map/convert_element_type | solution.py:58
  58.4 39.6 %conditional.4 = (f32[64,4096]{1,0:T(8,128)S(1)}) conditional(s32[]{:T(128)} %convert_element_type.125, () %tuple.25, (f32[64,4096]{1,0:T(8,128)S(1)}, f32[64,4096]{1,0:T(8,128)S(1)}, f32[64,64]{1,0:T(8,128)S(1)}, f32[128,128]{1,0:T(8,128)S(1)}, f32[64,64]{1,0:T(8,128)S(1)}, /*index=5*/f32[64,4096]{1,0:T(8,128)}, f32[64,64]{1,0:T(8,128)S(1)}, ...), branch_computations={%region_2.3_spmd, %region_3.4_spmd} | conditional | flops 1611137024 | bytes 31653896 | solution.py:60
  60.1 1.1 reshape.200
  61.2 2.2 fusion.23
  63.4 1.7 reshape.201
  65.1 6.4 %convolution_bitcast_fusion.7 = f32[64,64,64]{1,2,0:T(8,128)} fusion(f32[64,64,64]{2,1,0:T(8,128)} %reshape.201, f32[64,64]{1,0:T(8,128)S(1)} %get-tuple-element.76), kind=kOutput, calls=%fused_computation.11 | convolution fusion | flops 201326592 | bytes 2113536 | tf_op jit(solution)/shard_map/cond/branch_1_fun/ky,xyz->xkz/dot_general | solution.py:38
  71.4 3.1 %copy.41 = f32[64,64,64]{2,1,0:T(8,128)} copy(f32[64,64,64]{1,2,0:T(8,128)} %convolution_bitcast_fusion.7) | data formatting | bytes 2097152 | tf_op jit(solution)/shard_map/cond/branch_1_fun/ky,xyz->xkz/transpose | solution.py:38
  74.5 2.1 reshape.202
  76.6 3.4 %convolution_bitcast_fusion.4 = f32[64,4096]{1,0:T(8,128)} fusion(f32[64,64]{1,0:T(8,128)S(1)} %get-tuple-element.76, f32[64,4096]{1,0:T(8,128)S(1)} %reshape.202, f32[64,4096]{1,0:T(8,128)} %get-tuple-element.73), kind=kOutput, calls=%fused_computation.8 | convolution fusion | flops 201588736 | bytes 3162112 | tf_op jit(solution)/shard_map/cond/branch_1_fun/dot_general | solution.py:36
  80.1 2.4 reshape.203
  82.5 2.2 fusion.24
  84.7 1.7 reshape.204
  86.3 6.4 %convolution_bitcast_fusion.6 = f32[64,64,64]{1,2,0:T(8,128)} fusion(f32[64,64,64]{2,1,0:T(8,128)} %reshape.204, f32[64,64]{1,0:T(8,128)S(1)} %get-tuple-element.76), kind=kOutput, calls=%fused_computation.10 | convolution fusion | flops 201326592 | bytes 2113536 | tf_op jit(solution)/shard_map/cond/branch_1_fun/ky,xyz->xkz/dot_general | solution.py:38
  92.7 2.9 %copy.43 = f32[64,64,64]{2,1,0:T(8,128)} copy(f32[64,64,64]{1,2,0:T(8,128)} %convolution_bitcast_fusion.6) | data formatting | bytes 2097152 | tf_op jit(solution)/shard_map/cond/branch_1_fun/ky,xyz->xkz/transpose | solution.py:38
  95.6 2.1 reshape.205
  98.8 9.7 %convert_reduce_fusion.2 = f32[262144]{0:T(1024)S(1)} fusion(bf16[1,262144]{1,0:T(2,128)(2,1)} %collective-permute-done), kind=kLoop, calls=%fused_computation.29 | loop fusion | flops 262144 | bytes 1572864 | tf_op jit(solution)/shard_map/convert_element_type | solution.py:58
  108.8 39.2 %conditional.3 = (f32[64,4096]{1,0:T(8,128)S(1)}) conditional(s32[]{:T(128)} %convert_element_type.116, () %tuple.23, (f32[64,4096]{1,0:T(8,128)S(1)}, f32[64,4096]{1,0:T(8,128)S(1)}, f32[64,64]{1,0:T(8,128)S(1)}, f32[128,128]{1,0:T(8,128)S(1)}, f32[64,64]{1,0:T(8,128)S(1)}, /*index=5*/f32[64,4096]{1,0:T(8,128)}, f32[64,64]{1,0:T(8,128)S(1)}, ...), branch_computations={%region_0.1_spmd, %region_1.2_spmd} | conditional | flops 1611137024 | bytes 31653896 | solution.py:60
  109.9 1.1 reshape.194
  111.0 2.2 fusion.21
  113.2 1.7 reshape.195
  114.9 6.4 %convolution_bitcast_fusion.3 = f32[64,64,64]{1,2,0:T(8,128)} fusion(f32[64,64,64]{2,1,0:T(8,128)} %reshape.195, f32[64,64]{1,0:T(8,128)S(1)} %get-tuple-element.55), kind=kOutput, calls=%fused_computation.3 | convolution fusion | flops 201326592 | bytes 2113536 | tf_op jit(solution)/shard_map/cond/branch_1_fun/ky,xyz->xkz/dot_general | solution.py:38
  121.3 3.3 %copy.37 = f32[64,64,64]{2,1,0:T(8,128)} copy(f32[64,64,64]{1,2,0:T(8,128)} %convolution_bitcast_fusion.3) | data formatting | bytes 2097152 | tf_op jit(solution)/shard_map/cond/branch_1_fun/ky,xyz->xkz/transpose | solution.py:38
  124.6 2.1 reshape.196
  126.7 3.4 %convolution_bitcast_fusion = f32[64,4096]{1,0:T(8,128)} fusion(f32[64,64]{1,0:T(8,128)S(1)} %get-tuple-element.55, f32[64,4096]{1,0:T(8,128)S(1)} %reshape.196, f32[64,4096]{1,0:T(8,128)} %get-tuple-element.52), kind=kOutput, calls=%fused_computation | convolution fusion | flops 201588736 | bytes 3162112 | tf_op jit(solution)/shard_map/cond/branch_1_fun/dot_general | solution.py:36
  130.1 2.4 reshape.197
  132.5 2.2 fusion.22
  134.7 1.7 reshape.198
  136.4 6.4 %convolution_bitcast_fusion.2 = f32[64,64,64]{1,2,0:T(8,128)} fusion(f32[64,64,64]{2,1,0:T(8,128)} %reshape.198, f32[64,64]{1,0:T(8,128)S(1)} %get-tuple-element.55), kind=kOutput, calls=%fused_computation.2 | convolution fusion | flops 201326592 | bytes 2113536 | tf_op jit(solution)/shard_map/cond/branch_1_fun/ky,xyz->xkz/dot_general | solution.py:38
  142.7 2.9 %copy.39 = f32[64,64,64]{2,1,0:T(8,128)} copy(f32[64,64,64]{1,2,0:T(8,128)} %convolution_bitcast_fusion.2) | data formatting | bytes 2097152 | tf_op jit(solution)/shard_map/cond/branch_1_fun/ky,xyz->xkz/transpose | solution.py:38
  145.6 2.1 reshape.199
  148.9 9.7 %convert_reduce_fusion = f32[262144]{0:T(1024)S(1)} fusion(bf16[1,262144]{1,0:T(2,128)(2,1)} %collective-permute-done.2), kind=kLoop, calls=%fused_computation.27 | loop fusion | flops 262144 | bytes 1572864 | tf_op jit(solution)/shard_map/convert_element_type | solution.py:58
  158.8 35.7 %conditional.5 = (f32[64,4096]{1,0:T(8,128)S(1)}) conditional(s32[]{:T(128)} %convert_element_type.130, () %tuple.27, (f32[64,4096]{1,0:T(8,128)S(1)}, f32[64,4096]{1,0:T(8,128)S(1)}, f32[64,64]{1,0:T(8,128)S(1)}, f32[128,128]{1,0:T(8,128)S(1)}, f32[64,64]{1,0:T(8,128)S(1)}, /*index=5*/f32[64,4096]{1,0:T(8,128)}, f32[64,64]{1,0:T(8,128)S(1)}, ...), branch_computations={%region_4.5_spmd, %region_5.6_spmd} | conditional | flops 1611137024 | bytes 35848228 | solution.py:60
  160.0 1.1 reshape.206
  161.1 2.2 fusion.25
  163.3 1.7 reshape.207
  164.9 6.4 %convolution_bitcast_fusion.11 = f32[64,64,64]{1,2,0:T(8,128)} fusion(f32[64,64,64]{2,1,0:T(8,128)} %reshape.207, f32[64,64]{1,0:T(8,128)S(1)} %get-tuple-element.85), kind=kOutput, calls=%fused_computation.19 | convolution fusion | flops 201326592 | bytes 2113536 | tf_op jit(solution)/shard_map/cond/branch_1_fun/ky,xyz->xkz/dot_general | solution.py:38
  171.3 3.1 %copy.45 = f32[64,64,64]{2,1,0:T(8,128)} copy(f32[64,64,64]{1,2,0:T(8,128)} %convolution_bitcast_fusion.11) | data formatting | bytes 2097152 | tf_op jit(solution)/shard_map/cond/branch_1_fun/ky,xyz->xkz/transpose | solution.py:38
  174.4 2.2 reshape.208
  176.6 2.2 convolution_bitcast_fusion.8
  178.8 1.4 reshape.209
  181.2 1.7 reshape.210
  182.8 6.4 %convolution_bitcast_fusion.10 = f32[64,64,64]{1,2,0:T(8,128)} fusion(f32[64,64,64]{2,1,0:T(8,128)} %reshape.210, f32[64,64]{1,0:T(8,128)S(1)} %get-tuple-element.85), kind=kOutput, calls=%fused_computation.18 | convolution fusion | flops 201326592 | bytes 2113536 | tf_op jit(solution)/shard_map/cond/branch_1_fun/ky,xyz->xkz/dot_general | solution.py:38
  189.2 2.9 %copy.47 = f32[64,64,64]{2,1,0:T(8,128)} copy(f32[64,64,64]{1,2,0:T(8,128)} %convolution_bitcast_fusion.10) | data formatting | bytes 2097152 | tf_op jit(solution)/shard_map/cond/branch_1_fun/ky,xyz->xkz/transpose | solution.py:38
  192.1 2.1 reshape.211
  195.7 2.1 add_convert_fusion
  197.9 1.2 reshape.216
  199.0 6.2 %all-to-all-start = ((bf16[1,1,8,4,8192]{4,3,1,0,2:T(4,128)(2,1)}), bf16[1,1,8,4,8192]{4,3,1,0,2:T(4,128)(2,1)S(1)}, u32[]{:S(2)}, u32[]{:S(2)}) async-start(bf16[1,1,8,4,8192]{4,3,1,0,2:T(4,128)(2,1)} %reshape.216), calls=%async_computation | async-start | bytes 1048576 | tf_op jit(solution)/shard_map/all_to_all | solution.py:79
  205.3 2.1 copy.50
  207.4 10.4 %all-to-all-done = bf16[1,1,8,4,8192]{4,3,1,0,2:T(4,128)(2,1)S(1)} async-done(((bf16[1,1,8,4,8192]{4,3,1,0,2:T(4,128)(2,1)}), bf16[1,1,8,4,8192]{4,3,1,0,2:T(4,128)(2,1)S(1)}, u32[]{:S(2)}, u32[]{:S(2)}) %all-to-all-start) | async-done | bytes 524320 | tf_op jit(solution)/shard_map/all_to_all | solution.py:79
  217.8 3.5 %all-to-all-start.3 = ((bf16[8,1,1,4,8192]{4,0,2,1,3:T(8,128)(2,1)}), bf16[8,1,1,4,8192]{4,0,2,1,3:T(8,128)(2,1)S(1)}, u32[]{:S(2)}, u32[]{:S(2)}) async-start(bf16[8,1,1,4,8192]{4,0,2,1,3:T(8,128)(2,1)} %copy.50), calls=%async_computation.3 | async-start | bytes 1048576 | tf_op jit(solution)/shard_map/all_to_all | solution.py:71
  222.4 7.7 %all-to-all-done.3 = bf16[8,1,1,4,8192]{4,0,2,1,3:T(8,128)(2,1)S(1)} async-done(((bf16[8,1,1,4,8192]{4,0,2,1,3:T(8,128)(2,1)}), bf16[8,1,1,4,8192]{4,0,2,1,3:T(8,128)(2,1)S(1)}, u32[]{:S(2)}, u32[]{:S(2)}) %all-to-all-start.3) | async-done | bytes 524320 | tf_op jit(solution)/shard_map/all_to_all | solution.py:71
  230.1 3.5 %all-to-all-start.1 = ((bf16[8,1,1,4,8192]{4,0,2,1,3:T(8,128)(2,1)}), bf16[8,1,1,4,8192]{4,0,2,1,3:T(8,128)(2,1)S(1)}, u32[]{:S(2)}, u32[]{:S(2)}) async-start(bf16[8,1,1,4,8192]{4,0,2,1,3:T(8,128)(2,1)} %copy.48), calls=%async_computation.1 | async-start | bytes 1048576 | tf_op jit(solution)/shard_map/all_to_all | solution.py:78
  234.1 8.2 %all-to-all-done.1 = bf16[8,1,1,4,8192]{4,0,2,1,3:T(8,128)(2,1)S(1)} async-done(((bf16[8,1,1,4,8192]{4,0,2,1,3:T(8,128)(2,1)}), bf16[8,1,1,4,8192]{4,0,2,1,3:T(8,128)(2,1)S(1)}, u32[]{:S(2)}, u32[]{:S(2)}) %all-to-all-start.1) | async-done | bytes 524320 | tf_op jit(solution)/shard_map/all_to_all | solution.py:78
  243.2 38.5 %psum.7 = f32[32,32]{0,1:T(8,128)S(1)} all-reduce(f32[32,32]{0,1:T(8,128)S(1)} %fusion.12), channel_id=1, replica_groups=mesh['band'=8,'pair'=4] {'band','pair'}, use_global_device_ids=true, to_apply=%region_6.7 | all-reduce | flops 1024 | bytes 8192 | tf_op jit(solution)/shard_map/psum | solution.py:92
  281.6 1.5 convolution_subtract_fusion
  (45 shorter events, 14.2 us)
Async XLA Ops:
  0.0 24.6 %copy-start.1 = (bf16[1,262144]{1,0:T(2,128)(2,1)S(1)}, bf16[1,262144]{1,0:T(2,128)(2,1)}, u32[]{:S(2)}) copy-start(bf16[1,262144]{1,0:T(2,128)(2,1)} %param.8) | copy-start | bytes 1572868
  0.0 48.4 %collective-permute-start.1 = (bf16[1,262144]{1,0:T(2,128)(2,1)}, bf16[1,262144]{1,0:T(2,128)(2,1)}, u32[]{:S(2)}, u32[]{:S(2)}) collective-permute-start(bf16[1,262144]{1,0:T(2,128)(2,1)} %param.8), channel_id=1, source_target_pairs={{0,8},{4,12},{8,0},{12,4},{16,24},{20,28},{24,16},{28,20},{1,9},{5... | collective-permute-start | bytes 1572872 | tf_op jit(solution)/shard_map/ppermute | solution.py:16
  3.1 95.8 %collective-permute-start = (bf16[1,262144]{1,0:T(2,128)(2,1)}, bf16[1,262144]{1,0:T(2,128)(2,1)}, u32[]{:S(2)}, u32[]{:S(2)}) collective-permute-start(bf16[1,262144]{1,0:T(2,128)(2,1)} %param.8), channel_id=1, source_target_pairs={{0,4},{4,0},{8,12},{12,8},{16,20},{20,16},{24,28},{28,24},{1,5},{5... | collective-permute-start | bytes 1572872 | tf_op jit(solution)/shard_map/ppermute | solution.py:16
  4.6 144.3 %collective-permute-start.2 = (bf16[1,262144]{1,0:T(2,128)(2,1)}, bf16[1,262144]{1,0:T(2,128)(2,1)}, u32[]{:S(2)}, u32[]{:S(2)}) collective-permute-start(bf16[1,262144]{1,0:T(2,128)(2,1)} %param.8), channel_id=1, source_target_pairs={{0,16},{4,20},{8,24},{12,28},{16,0},{20,4},{24,8},{28,12},{1,17},{... | collective-permute-start | bytes 1572872 | tf_op jit(solution)/shard_map/ppermute | solution.py:16
  20.0 179.0 %all-to-all-start.2 = ((bf16[1,1,8,4,8192]{4,3,1,0,2:T(4,128)(2,1)}), bf16[1,1,8,4,8192]{4,3,1,0,2:T(4,128)(2,1)}, u32[]{:S(2)}, u32[]{:S(2)}) async-start(bf16[1,1,8,4,8192]{4,3,1,0,2:T(4,128)(2,1)} %reshape.218), calls=%async_computation.2 | async-start | bytes 1048576 | tf_op jit(solution)/shard_map/all_to_all | solution.py:72
  35.4 3.3 %copy-start.5 = (s32[1,3]{1,0:T(1,128)S(1)}, s32[1,3]{1,0:T(1,128)}, u32[]{:S(2)}) copy-start(s32[1,3]{1,0:T(1,128)} %param.9) | copy-start | bytes 40
  37.1 4.1 %copy-start = (f32[64,4096]{1,0:T(8,128)S(1)}, f32[64,4096]{1,0:T(8,128)}, u32[]{:S(2)}) copy-start(f32[64,4096]{1,0:T(8,128)} %add.210) | copy-start | bytes 3145732
  174.4 2.2 copy-start.4
  194.5 1.0 copy-start.2
  194.5 1.2 copy-start.3
  199.0 18.8 %all-to-all-start = ((bf16[1,1,8,4,8192]{4,3,1,0,2:T(4,128)(2,1)}), bf16[1,1,8,4,8192]{4,3,1,0,2:T(4,128)(2,1)S(1)}, u32[]{:S(2)}, u32[]{:S(2)}) async-start(bf16[1,1,8,4,8192]{4,3,1,0,2:T(4,128)(2,1)} %reshape.216), calls=%async_computation | async-start | bytes 1048576 | tf_op jit(solution)/shard_map/all_to_all | solution.py:79
  217.8 12.3 %all-to-all-start.3 = ((bf16[8,1,1,4,8192]{4,0,2,1,3:T(8,128)(2,1)}), bf16[8,1,1,4,8192]{4,0,2,1,3:T(8,128)(2,1)S(1)}, u32[]{:S(2)}, u32[]{:S(2)}) async-start(bf16[8,1,1,4,8192]{4,0,2,1,3:T(8,128)(2,1)} %copy.50), calls=%async_computation.3 | async-start | bytes 1048576 | tf_op jit(solution)/shard_map/all_to_all | solution.py:71
  230.1 12.3 %all-to-all-start.1 = ((bf16[8,1,1,4,8192]{4,0,2,1,3:T(8,128)(2,1)}), bf16[8,1,1,4,8192]{4,0,2,1,3:T(8,128)(2,1)S(1)}, u32[]{:S(2)}, u32[]{:S(2)}) async-start(bf16[8,1,1,4,8192]{4,0,2,1,3:T(8,128)(2,1)} %copy.48), calls=%async_computation.1 | async-start | bytes 1048576 | tf_op jit(solution)/shard_map/all_to_all | solution.py:78
where the time goes:
time: 289 us; the launch traced here: 283 us
  matrix products  64.3 us (22%)
  local copies, waits for them, and re-layouts  63.2 us (22%)
  other arithmetic  56.3 us (19%)
  blocking collectives  38.5 us (13%)
  waiting for transfers between devices  32.5 us (11%)
  starting transfers between devices  24.8 us (9%)
    psum x1, blocking collectives, on_device(): lax.psum(partial_intersection * (1.0 / NG3), ('band', 'pair'))  38.5 us
    dot_general x6, matrix products, sine_transform(): jnp.einsum('ky,xyz->xkz', table, field.reshape(size, size, size), precisi...  38.2 us
    convert_element_type x3, other arithmetic, on_device(): other = arrived.reshape(NG, NG * NG).astype(jnp.float32)  29.2 us
    transpose x6, local copies, waits for them, and re-layouts, sine_transform(): jnp.einsum('ky,xyz->xkz', table, field.reshape(size, size, size), precisi...  18.1 us
    reshape x6, local copies, waits for them, and re-layouts, sine_transform(): return field.reshape(size, size * size)  12.8 us
    dot_general x6, matrix products, sine_transform(): field = jnp.dot(table, field, precision=highest)  12.4 us
    dot_general x6, matrix products, sine_transform(): field = jnp.dot(field.reshape(-1, 2 * size), doubled, precision=highest)  11.9 us
    unnamed x1, other arithmetic  11.9 us
  transfers between devices with their start and end apart: 7, of which 4 were waited for; matrix products, arithmetic and copies ran while one was open for 64% of the time, Pallas kernels for 0%

commit v1 on v0

--- a/solution.py
+++ b/solution.py
@@ -89,7 +89,9 @@
     partial_intersection = lax.dot_general(
         phi_slab, applied_slab, (((1,), (1,)), ((), ())), preferred_element_type=jnp.float32
     )
-    intersection = lax.psum(partial_intersection * (1.0 / NG3), ("band", "pair"))
+    intersection = jnp.sum(
+        lax.all_gather(partial_intersection * (1.0 / NG3), ("band", "pair")), axis=0
+    )
     removed = lax.dot_general(
         intersection,
         phi_slab.astype(jnp.float32),

time: 289 us -> 291 us (level)
    all_gather x0 -> x1, blocking collectives: none -> 40 us  [on_device(): lax.all_gather(partial_intersection * (1.0 / NG3), ('band', 'pair'))]
    psum x1 -> x0, blocking collectives: 38.5 us -> none  [on_device(): lax.psum(partial_intersection * (1.0 / NG3), ('band', 'pair'))]
    unnamed x1 -> x2, other arithmetic: 11.9 us -> 12 us
  transfers between devices with their start and end apart: 7 -> 7, of which waited for: 4 -> 4; matrix products, arithmetic and copies ran while one was open for 64% -> 63% of each run, Pallas kernels for 0% -> 0%
where the time goes in v1:
time: 291 us; the launch traced here: 285 us
  matrix products  64.4 us (22%)
  local copies, waits for them, and re-layouts  63.3 us (22%)
  other arithmetic  56.4 us (19%)
  blocking collectives  40 us (14%)
  waiting for transfers between devices  32.5 us (11%)
  starting transfers between devices  24.8 us (9%)
    all_gather x1, blocking collectives, on_device(): lax.all_gather(partial_intersection * (1.0 / NG3), ('band', 'pair'))  40 us
    dot_general x6, matrix products, sine_transform(): jnp.einsum('ky,xyz->xkz', table, field.reshape(size, size, size), precisi...  38.2 us
    convert_element_type x3, other arithmetic, on_device(): other = arrived.reshape(NG, NG * NG).astype(jnp.float32)  29.2 us
    transpose x6, local copies, waits for them, and re-layouts, sine_transform(): jnp.einsum('ky,xyz->xkz', table, field.reshape(size, size, size), precisi...  18.1 us
    reshape x6, local copies, waits for them, and re-layouts, sine_transform(): return field.reshape(size, size * size)  12.8 us
    dot_general x6, matrix products, sine_transform(): field = jnp.dot(table, field, precision=highest)  12.4 us
    unnamed x2, other arithmetic  12 us
    dot_general x6, matrix products, sine_transform(): field = jnp.dot(field.reshape(-1, 2 * size), doubled, precision=highest)  11.9 us
  transfers between devices with their start and end apart: 7, of which 4 were waited for; matrix products, arithmetic and copies ran while one was open for 63% of the time, Pallas kernels for 0%

profile of v1, /device:TPU:0, one launch (start us, length us, event | category | flops | bytes accessed | tf_op | source)
XLA Modules:
  0.0 285.2 jit_solution(16599259336757993321)
XLA Ops:
  0.0 3.1 %collective-permute-start.1 = (bf16[1,262144]{1,0:T(2,128)(2,1)}, bf16[1,262144]{1,0:T(2,128)(2,1)}, u32[]{:S(2)}, u32[]{:S(2)}) collective-permute-start(bf16[1,262144]{1,0:T(2,128)(2,1)} %param.8), channel_id=1, source_target_pairs={{0,8},{4,12},{8,0},{12,4},{16,24},{20,28},{24,16},{28,20},{1,9},{5... | collective-permute-start | bytes 1572872 | tf_op jit(solution)/shard_map/ppermute | solution.py:16
  3.1 1.5 collective-permute-start
  4.6 2.6 collective-permute-start.2
  7.2 11.9 %reduce.4 = bf16[262144]{0:T(1024)(128)(2,1)S(1)} reduce(bf16[1,262144]{1,0:T(2,128)(2,1)} %param.8, bf16[]{:T(256)} %constant.51), dimensions={0}, to_apply=%param.8.reduce_sub_computation | reduce | bytes 1048578 | tf_op args[0]
  20.0 4.5 %all-to-all-start.2 = ((bf16[1,1,8,4,8192]{4,3,1,0,2:T(4,128)(2,1)}), bf16[1,1,8,4,8192]{4,3,1,0,2:T(4,128)(2,1)}, u32[]{:S(2)}, u32[]{:S(2)}) async-start(bf16[1,1,8,4,8192]{4,3,1,0,2:T(4,128)(2,1)} %reshape.218), calls=%async_computation.2 | async-start | bytes 1048576 | tf_op jit(solution)/shard_map/all_to_all | solution.py:72
  24.6 9.7 %convert_reduce_fusion.3 = f32[262144]{0:T(1024)} fusion(bf16[1,262144]{1,0:T(2,128)(2,1)S(1)} %copy-done.1), kind=kLoop, calls=%fused_computation.30 | loop fusion | flops 262144 | bytes 1572864 | tf_op jit(solution)/shard_map/convert_element_type | solution.py:53
  35.4 1.7 add.208
  37.2 1.5 reshape.220
  42.3 6.1 %collective-permute-done.1 = bf16[1,262144]{1,0:T(2,128)(2,1)} collective-permute-done((bf16[1,262144]{1,0:T(2,128)(2,1)}, bf16[1,262144]{1,0:T(2,128)(2,1)}, u32[]{:S(2)}, u32[]{:S(2)}) %collective-permute-start.1) | collective-permute-done | bytes 524320 | tf_op jit(solution)/shard_map/ppermute | solution.py:16
  48.4 9.7 %convert_reduce_fusion.1 = f32[262144]{0:T(1024)S(1)} fusion(bf16[1,262144]{1,0:T(2,128)(2,1)} %collective-permute-done.1), kind=kLoop, calls=%fused_computation.28 | loop fusion | flops 262144 | bytes 1572864 | tf_op jit(solution)/shard_map/convert_element_type | solution.py:58
  58.4 39.6 %conditional.4 = (f32[64,4096]{1,0:T(8,128)S(1)}) conditional(s32[]{:T(128)} %convert_element_type.125, () %tuple.25, (f32[64,4096]{1,0:T(8,128)S(1)}, f32[64,4096]{1,0:T(8,128)S(1)}, f32[64,64]{1,0:T(8,128)S(1)}, f32[128,128]{1,0:T(8,128)S(1)}, f32[64,64]{1,0:T(8,128)S(1)}, /*index=5*/f32[64,4096]{1,0:T(8,128)}, f32[64,64]{1,0:T(8,128)S(1)}, ...), branch_computations={%region_2.3_spmd, %region_3.4_spmd} | conditional | flops 1611137024 | bytes 31653896 | solution.py:60
  60.1 1.1 reshape.200
  61.2 2.2 fusion.23
  63.4 1.7 reshape.201
  65.1 6.4 %convolution_bitcast_fusion.7 = f32[64,64,64]{1,2,0:T(8,128)} fusion(f32[64,64,64]{2,1,0:T(8,128)} %reshape.201, f32[64,64]{1,0:T(8,128)S(1)} %get-tuple-element.76), kind=kOutput, calls=%fused_computation.11 | convolution fusion | flops 201326592 | bytes 2113536 | tf_op jit(solution)/shard_map/cond/branch_1_fun/ky,xyz->xkz/dot_general | solution.py:38
  71.4 3.1 %copy.43 = f32[64,64,64]{2,1,0:T(8,128)} copy(f32[64,64,64]{1,2,0:T(8,128)} %convolution_bitcast_fusion.7) | data formatting | bytes 2097152 | tf_op jit(solution)/shard_map/cond/branch_1_fun/ky,xyz->xkz/transpose | solution.py:38
  74.5 2.1 reshape.202
  76.6 3.4 %convolution_bitcast_fusion.4 = f32[64,4096]{1,0:T(8,128)} fusion(f32[64,64]{1,0:T(8,128)S(1)} %get-tuple-element.76, f32[64,4096]{1,0:T(8,128)S(1)} %reshape.202, f32[64,4096]{1,0:T(8,128)} %get-tuple-element.73), kind=kOutput, calls=%fused_computation.8 | convolution fusion | flops 201588736 | bytes 3162112 | tf_op jit(solution)/shard_map/cond/branch_1_fun/dot_general | solution.py:36
  80.1 2.4 reshape.203
  82.5 2.2 fusion.24
  84.7 1.7 reshape.204
  86.3 6.4 %convolution_bitcast_fusion.6 = f32[64,64,64]{1,2,0:T(8,128)} fusion(f32[64,64,64]{2,1,0:T(8,128)} %reshape.204, f32[64,64]{1,0:T(8,128)S(1)} %get-tuple-element.76), kind=kOutput, calls=%fused_computation.10 | convolution fusion | flops 201326592 | bytes 2113536 | tf_op jit(solution)/shard_map/cond/branch_1_fun/ky,xyz->xkz/dot_general | solution.py:38
  92.7 2.9 %copy.45 = f32[64,64,64]{2,1,0:T(8,128)} copy(f32[64,64,64]{1,2,0:T(8,128)} %convolution_bitcast_fusion.6) | data formatting | bytes 2097152 | tf_op jit(solution)/shard_map/cond/branch_1_fun/ky,xyz->xkz/transpose | solution.py:38
  95.6 2.1 reshape.205
  98.8 9.7 %convert_reduce_fusion.2 = f32[262144]{0:T(1024)S(1)} fusion(bf16[1,262144]{1,0:T(2,128)(2,1)} %collective-permute-done), kind=kLoop, calls=%fused_computation.29 | loop fusion | flops 262144 | bytes 1572864 | tf_op jit(solution)/shard_map/convert_element_type | solution.py:58
  108.8 39.2 %conditional.3 = (f32[64,4096]{1,0:T(8,128)S(1)}) conditional(s32[]{:T(128)} %convert_element_type.116, () %tuple.23, (f32[64,4096]{1,0:T(8,128)S(1)}, f32[64,4096]{1,0:T(8,128)S(1)}, f32[64,64]{1,0:T(8,128)S(1)}, f32[128,128]{1,0:T(8,128)S(1)}, f32[64,64]{1,0:T(8,128)S(1)}, /*index=5*/f32[64,4096]{1,0:T(8,128)}, f32[64,64]{1,0:T(8,128)S(1)}, ...), branch_computations={%region_0.1_spmd, %region_1.2_spmd} | conditional | flops 1611137024 | bytes 31653896 | solution.py:60
  109.9 1.1 reshape.194
  111.0 2.2 fusion.21
  113.2 1.7 reshape.195
  114.9 6.4 %convolution_bitcast_fusion.3 = f32[64,64,64]{1,2,0:T(8,128)} fusion(f32[64,64,64]{2,1,0:T(8,128)} %reshape.195, f32[64,64]{1,0:T(8,128)S(1)} %get-tuple-element.55), kind=kOutput, calls=%fused_computation.3 | convolution fusion | flops 201326592 | bytes 2113536 | tf_op jit(solution)/shard_map/cond/branch_1_fun/ky,xyz->xkz/dot_general | solution.py:38
  121.3 3.3 %copy.39 = f32[64,64,64]{2,1,0:T(8,128)} copy(f32[64,64,64]{1,2,0:T(8,128)} %convolution_bitcast_fusion.3) | data formatting | bytes 2097152 | tf_op jit(solution)/shard_map/cond/branch_1_fun/ky,xyz->xkz/transpose | solution.py:38
  124.6 2.1 reshape.196
  126.7 3.4 %convolution_bitcast_fusion = f32[64,4096]{1,0:T(8,128)} fusion(f32[64,64]{1,0:T(8,128)S(1)} %get-tuple-element.55, f32[64,4096]{1,0:T(8,128)S(1)} %reshape.196, f32[64,4096]{1,0:T(8,128)} %get-tuple-element.52), kind=kOutput, calls=%fused_computation | convolution fusion | flops 201588736 | bytes 3162112 | tf_op jit(solution)/shard_map/cond/branch_1_fun/dot_general | solution.py:36
  130.1 2.4 reshape.197
  132.5 2.2 fusion.22
  134.7 1.7 reshape.198
  136.4 6.4 %convolution_bitcast_fusion.2 = f32[64,64,64]{1,2,0:T(8,128)} fusion(f32[64,64,64]{2,1,0:T(8,128)} %reshape.198, f32[64,64]{1,0:T(8,128)S(1)} %get-tuple-element.55), kind=kOutput, calls=%fused_computation.2 | convolution fusion | flops 201326592 | bytes 2113536 | tf_op jit(solution)/shard_map/cond/branch_1_fun/ky,xyz->xkz/dot_general | solution.py:38
  142.7 2.9 %copy.41 = f32[64,64,64]{2,1,0:T(8,128)} copy(f32[64,64,64]{1,2,0:T(8,128)} %convolution_bitcast_fusion.2) | data formatting | bytes 2097152 | tf_op jit(solution)/shard_map/cond/branch_1_fun/ky,xyz->xkz/transpose | solution.py:38
  145.6 2.1 reshape.199
  148.9 9.7 %convert_reduce_fusion = f32[262144]{0:T(1024)S(1)} fusion(bf16[1,262144]{1,0:T(2,128)(2,1)} %collective-permute-done.2), kind=kLoop, calls=%fused_computation.27 | loop fusion | flops 262144 | bytes 1572864 | tf_op jit(solution)/shard_map/convert_element_type | solution.py:58
  158.8 35.7 %conditional.5 = (f32[64,4096]{1,0:T(8,128)S(1)}) conditional(s32[]{:T(128)} %convert_element_type.130, () %tuple.27, (f32[64,4096]{1,0:T(8,128)S(1)}, f32[64,4096]{1,0:T(8,128)S(1)}, f32[64,64]{1,0:T(8,128)S(1)}, f32[128,128]{1,0:T(8,128)S(1)}, f32[64,64]{1,0:T(8,128)S(1)}, /*index=5*/f32[64,4096]{1,0:T(8,128)}, f32[64,64]{1,0:T(8,128)S(1)}, ...), branch_computations={%region_4.5_spmd, %region_5.6_spmd} | conditional | flops 1611137024 | bytes 35848228 | solution.py:60
  160.0 1.1 reshape.206
  161.1 2.2 fusion.25
  163.3 1.7 reshape.207
  164.9 6.4 %convolution_bitcast_fusion.11 = f32[64,64,64]{1,2,0:T(8,128)} fusion(f32[64,64,64]{2,1,0:T(8,128)} %reshape.207, f32[64,64]{1,0:T(8,128)S(1)} %get-tuple-element.85), kind=kOutput, calls=%fused_computation.19 | convolution fusion | flops 201326592 | bytes 2113536 | tf_op jit(solution)/shard_map/cond/branch_1_fun/ky,xyz->xkz/dot_general | solution.py:38
  171.3 3.1 %copy.47 = f32[64,64,64]{2,1,0:T(8,128)} copy(f32[64,64,64]{1,2,0:T(8,128)} %convolution_bitcast_fusion.11) | data formatting | bytes 2097152 | tf_op jit(solution)/shard_map/cond/branch_1_fun/ky,xyz->xkz/transpose | solution.py:38
  174.4 2.2 reshape.208
  176.6 2.2 convolution_bitcast_fusion.8
  178.8 1.4 reshape.209
  181.2 1.7 reshape.210
  182.8 6.4 %convolution_bitcast_fusion.10 = f32[64,64,64]{1,2,0:T(8,128)} fusion(f32[64,64,64]{2,1,0:T(8,128)} %reshape.210, f32[64,64]{1,0:T(8,128)S(1)} %get-tuple-element.85), kind=kOutput, calls=%fused_computation.18 | convolution fusion | flops 201326592 | bytes 2113536 | tf_op jit(solution)/shard_map/cond/branch_1_fun/ky,xyz->xkz/dot_general | solution.py:38
  189.2 2.9 %copy.49 = f32[64,64,64]{2,1,0:T(8,128)} copy(f32[64,64,64]{1,2,0:T(8,128)} %convolution_bitcast_fusion.10) | data formatting | bytes 2097152 | tf_op jit(solution)/shard_map/cond/branch_1_fun/ky,xyz->xkz/transpose | solution.py:38
  192.1 2.1 reshape.211
  195.7 2.1 add_convert_fusion
  197.9 1.2 reshape.216
  199.0 6.2 %all-to-all-start = ((bf16[1,1,8,4,8192]{4,3,1,0,2:T(4,128)(2,1)}), bf16[1,1,8,4,8192]{4,3,1,0,2:T(4,128)(2,1)S(1)}, u32[]{:S(2)}, u32[]{:S(2)}) async-start(bf16[1,1,8,4,8192]{4,3,1,0,2:T(4,128)(2,1)} %reshape.216), calls=%async_computation | async-start | bytes 1048576 | tf_op jit(solution)/shard_map/all_to_all | solution.py:79
  205.3 2.1 copy.52
  207.4 10.4 %all-to-all-done = bf16[1,1,8,4,8192]{4,3,1,0,2:T(4,128)(2,1)S(1)} async-done(((bf16[1,1,8,4,8192]{4,3,1,0,2:T(4,128)(2,1)}), bf16[1,1,8,4,8192]{4,3,1,0,2:T(4,128)(2,1)S(1)}, u32[]{:S(2)}, u32[]{:S(2)}) %all-to-all-start) | async-done | bytes 524320 | tf_op jit(solution)/shard_map/all_to_all | solution.py:79
  217.8 3.5 %all-to-all-start.3 = ((bf16[8,1,1,4,8192]{4,0,2,1,3:T(8,128)(2,1)}), bf16[8,1,1,4,8192]{4,0,2,1,3:T(8,128)(2,1)S(1)}, u32[]{:S(2)}, u32[]{:S(2)}) async-start(bf16[8,1,1,4,8192]{4,0,2,1,3:T(8,128)(2,1)} %copy.52), calls=%async_computation.3 | async-start | bytes 1048576 | tf_op jit(solution)/shard_map/all_to_all | solution.py:71
  222.4 7.7 %all-to-all-done.3 = bf16[8,1,1,4,8192]{4,0,2,1,3:T(8,128)(2,1)S(1)} async-done(((bf16[8,1,1,4,8192]{4,0,2,1,3:T(8,128)(2,1)}), bf16[8,1,1,4,8192]{4,0,2,1,3:T(8,128)(2,1)S(1)}, u32[]{:S(2)}, u32[]{:S(2)}) %all-to-all-start.3) | async-done | bytes 524320 | tf_op jit(solution)/shard_map/all_to_all | solution.py:71
  230.1 3.5 %all-to-all-start.1 = ((bf16[8,1,1,4,8192]{4,0,2,1,3:T(8,128)(2,1)}), bf16[8,1,1,4,8192]{4,0,2,1,3:T(8,128)(2,1)S(1)}, u32[]{:S(2)}, u32[]{:S(2)}) async-start(bf16[8,1,1,4,8192]{4,0,2,1,3:T(8,128)(2,1)} %copy.50), calls=%async_computation.1 | async-start | bytes 1048576 | tf_op jit(solution)/shard_map/all_to_all | solution.py:78
  234.1 8.2 %all-to-all-done.1 = bf16[8,1,1,4,8192]{4,0,2,1,3:T(8,128)(2,1)S(1)} async-done(((bf16[8,1,1,4,8192]{4,0,2,1,3:T(8,128)(2,1)}), bf16[8,1,1,4,8192]{4,0,2,1,3:T(8,128)(2,1)S(1)}, u32[]{:S(2)}, u32[]{:S(2)}) %all-to-all-start.1) | async-done | bytes 524320 | tf_op jit(solution)/shard_map/all_to_all | solution.py:78
  243.2 40.0 %all-gather = f32[1024,32]{1,0:T(8,128)S(1)} all-gather(f32[32,32]{1,0:T(8,128)S(1)} %copy.54), channel_id=2, replica_groups=mesh['band'=8,'pair'=4] {'band','pair'}, dimensions={0}, use_global_device_ids=true | all-gather | bytes 135168 | tf_op jit(solution)/shard_map/all_gather | solution.py:93
  283.3 1.6 convolution_subtract_fusion
  (47 shorter events, 14.4 us)
Async XLA Ops:
  0.0 24.6 %copy-start.1 = (bf16[1,262144]{1,0:T(2,128)(2,1)S(1)}, bf16[1,262144]{1,0:T(2,128)(2,1)}, u32[]{:S(2)}) copy-start(bf16[1,262144]{1,0:T(2,128)(2,1)} %param.8) | copy-start | bytes 1572868
  0.0 48.4 %collective-permute-start.1 = (bf16[1,262144]{1,0:T(2,128)(2,1)}, bf16[1,262144]{1,0:T(2,128)(2,1)}, u32[]{:S(2)}, u32[]{:S(2)}) collective-permute-start(bf16[1,262144]{1,0:T(2,128)(2,1)} %param.8), channel_id=1, source_target_pairs={{0,8},{4,12},{8,0},{12,4},{16,24},{20,28},{24,16},{28,20},{1,9},{5... | collective-permute-start | bytes 1572872 | tf_op jit(solution)/shard_map/ppermute | solution.py:16
  3.1 95.8 %collective-permute-start = (bf16[1,262144]{1,0:T(2,128)(2,1)}, bf16[1,262144]{1,0:T(2,128)(2,1)}, u32[]{:S(2)}, u32[]{:S(2)}) collective-permute-start(bf16[1,262144]{1,0:T(2,128)(2,1)} %param.8), channel_id=1, source_target_pairs={{0,4},{4,0},{8,12},{12,8},{16,20},{20,16},{24,28},{28,24},{1,5},{5... | collective-permute-start | bytes 1572872 | tf_op jit(solution)/shard_map/ppermute | solution.py:16
  4.6 144.3 %collective-permute-start.2 = (bf16[1,262144]{1,0:T(2,128)(2,1)}, bf16[1,262144]{1,0:T(2,128)(2,1)}, u32[]{:S(2)}, u32[]{:S(2)}) collective-permute-start(bf16[1,262144]{1,0:T(2,128)(2,1)} %param.8), channel_id=1, source_target_pairs={{0,16},{4,20},{8,24},{12,28},{16,0},{20,4},{24,8},{28,12},{1,17},{... | collective-permute-start | bytes 1572872 | tf_op jit(solution)/shard_map/ppermute | solution.py:16
  20.0 179.0 %all-to-all-start.2 = ((bf16[1,1,8,4,8192]{4,3,1,0,2:T(4,128)(2,1)}), bf16[1,1,8,4,8192]{4,3,1,0,2:T(4,128)(2,1)}, u32[]{:S(2)}, u32[]{:S(2)}) async-start(bf16[1,1,8,4,8192]{4,3,1,0,2:T(4,128)(2,1)} %reshape.218), calls=%async_computation.2 | async-start | bytes 1048576 | tf_op jit(solution)/shard_map/all_to_all | solution.py:72
  35.4 3.3 %copy-start.5 = (s32[1,3]{1,0:T(1,128)S(1)}, s32[1,3]{1,0:T(1,128)}, u32[]{:S(2)}) copy-start(s32[1,3]{1,0:T(1,128)} %param.9) | copy-start | bytes 40
  37.1 4.1 %copy-start = (f32[64,4096]{1,0:T(8,128)S(1)}, f32[64,4096]{1,0:T(8,128)}, u32[]{:S(2)}) copy-start(f32[64,4096]{1,0:T(8,128)} %add.208) | copy-start | bytes 3145732
  174.4 2.2 copy-start.4
  194.5 1.0 copy-start.2
  194.5 1.2 copy-start.3
  199.0 18.8 %all-to-all-start = ((bf16[1,1,8,4,8192]{4,3,1,0,2:T(4,128)(2,1)}), bf16[1,1,8,4,8192]{4,3,1,0,2:T(4,128)(2,1)S(1)}, u32[]{:S(2)}, u32[]{:S(2)}) async-start(bf16[1,1,8,4,8192]{4,3,1,0,2:T(4,128)(2,1)} %reshape.216), calls=%async_computation | async-start | bytes 1048576 | tf_op jit(solution)/shard_map/all_to_all | solution.py:79
  217.8 12.3 %all-to-all-start.3 = ((bf16[8,1,1,4,8192]{4,0,2,1,3:T(8,128)(2,1)}), bf16[8,1,1,4,8192]{4,0,2,1,3:T(8,128)(2,1)S(1)}, u32[]{:S(2)}, u32[]{:S(2)}) async-start(bf16[8,1,1,4,8192]{4,0,2,1,3:T(8,128)(2,1)} %copy.52), calls=%async_computation.3 | async-start | bytes 1048576 | tf_op jit(solution)/shard_map/all_to_all | solution.py:71
  230.1 12.3 %all-to-all-start.1 = ((bf16[8,1,1,4,8192]{4,0,2,1,3:T(8,128)(2,1)}), bf16[8,1,1,4,8192]{4,0,2,1,3:T(8,128)(2,1)S(1)}, u32[]{:S(2)}, u32[]{:S(2)}) async-start(bf16[8,1,1,4,8192]{4,0,2,1,3:T(8,128)(2,1)} %copy.50), calls=%async_computation.1 | async-start | bytes 1048576 | tf_op jit(solution)/shard_map/all_to_all | solution.py:78
